TPU v7x, 256 devices: a whole 4x4x8 slice. The times are simulated.
256 devices in a mesh: band: 64 (over z, y, core), tile: 4 (over x).
Axes of the slice: x: 4, y: 4, z: 8, core: 2. Of those that a mesh axis runs over, the one named last changes fastest.
Arguments:
- src_field: bfloat16 [4, 32, 1048576], P(None, None, ('band', 'tile')), may hold values from 0.0009994507 to 1
- weights: bfloat16 [65536, 128, 128], P(('band', 'tile')), may hold values from 0 to 0.05625
- block_slab: int32 [65536], P(('band', 'tile')), may hold values from 0 to 127
- block_dest: int32 [65536, 1], P(('band', 'tile')), may hold values from 0 to 255; in each aligned block of 256 rows (0 to 255, 256 to 511, ...) at most 2 rows name the same one
- block_tile: int32 [65536], P(('band', 'tile')), may hold values from 0 to 31
- prior_total: float32 [32, 1048576], P(None, ('band', 'tile')), may hold values from 0.2 to 4
- gamma_shape: float32 [1048576], P(('band', 'tile')), may hold values from 1 to 10
- gamma_scale: float32 [1048576], P(('band', 'tile')), may hold values from 0.05 to 0.6
Outputs:
- season_total: float32 [32, 1048576], P(None, ('band', 'tile'))
- spi_index: float32 [32, 1048576], P(None, ('band', 'tile'))
Inputs may be any that keep to these rules, and one draw needn't show every extreme that they name: `block_dest`: among the 256 blocks of any one device, each destination is named by at most 2 blocks, a bound that some block reaches.
All inputs are finite; a program needn't handle non-finite values.
Results may differ from a plain program's by a relative error of at most 0.00085.
Values may be sent and summed in bfloat16 or wider, within the bound.
A program may use at most 128 MiB of HBM per device.

v0:
```python
import jax
import jax.numpy as jnp
from jax import lax
from jax.sharding import PartitionSpec as P

PROB_FLOOR = 0.001
CENTRAL_NUMER = (
    -39.69683028665376,
    220.9460984245205,
    -275.9285104469687,
    138.357751867269,
    -30.66479806614716,
    2.506628277459239,
)
CENTRAL_DENOM = (
    -54.47609879822406,
    161.5858368580409,
    -155.6989798598866,
    66.80131188771972,
    -13.28068155288572,
    1.0,
)
TAIL_NUMER = (
    -0.007784894002430293,
    -0.3223964580411365,
    -2.400758277161838,
    -2.549671010429402,
    4.374664141464968,
    2.938163982698783,
)
TAIL_DENOM = (0.007784695709041462, 0.3224671290700398, 2.445134137142996, 3.754408661907416, 1.0)


def horner(coeffs, value):
    total = jnp.zeros_like(value) + coeffs[0]
    for coeff in coeffs[1:]:
        total = total * value + coeff
    return total


def normal_quantile(prob):
    centred = prob - 0.5
    square = centred * centred
    middle = centred * horner(CENTRAL_NUMER, square) / horner(CENTRAL_DENOM, square)
    lower_root = jnp.sqrt(-2.0 * jnp.log(prob))
    lower = horner(TAIL_NUMER, lower_root) / horner(TAIL_DENOM, lower_root)
    upper_root = jnp.sqrt(-2.0 * jnp.log(1.0 - prob))
    upper = -horner(TAIL_NUMER, upper_root) / horner(TAIL_DENOM, upper_root)
    result = jnp.where(prob < 0.02425, lower, middle)
    return jnp.where(prob > 0.97575, upper, result)


def lower_gamma(shape, value):
    border = shape + 1.0
    small_x = jnp.minimum(value, border)
    large_x = jnp.maximum(value, border)

    def series_step(index, carry):
        term, total = carry
        term = term * small_x / (shape + index)
        return (term, total + term)

    first = 1.0 / shape
    _, series = lax.fori_loop(1, 65, series_step, (first, first))
    series_value = series * jnp.exp(-small_x + shape * jnp.log(small_x) - lax.lgamma(shape))
    start_b = large_x + 1.0 - shape
    start_c = jnp.zeros_like(large_x) + 1e30
    start_d = 1.0 / start_b

    def fraction_step(index, carry):
        denom_b, lentz_c, lentz_d, accum = carry
        step_a = -index * (index - shape)
        denom_b = denom_b + 2.0
        lentz_d = 1.0 / (step_a * lentz_d + denom_b)
        lentz_c = denom_b + step_a / lentz_c
        return (denom_b, lentz_c, lentz_d, accum * lentz_d * lentz_c)

    _, _, _, fraction = lax.fori_loop(1, 65, fraction_step, (start_b, start_c, start_d, start_d))
    upper_value = fraction * jnp.exp(-large_x + shape * jnp.log(large_x) - lax.lgamma(shape))
    return jnp.where(value < border, series_value, 1.0 - upper_value)


def rank_within(owner_ids, groups):
    onehot = (owner_ids[:, None] == jnp.arange(groups, dtype=jnp.int32)[None, :]).astype(jnp.int32)
    before = jnp.cumsum(onehot, axis=0) - onehot
    return jnp.sum(before * onehot, axis=1)


def shards(
    src_field, weights, block_slab, block_dest, block_tile, prior_total, gamma_shape, gamma_scale
):
    band_count = lax.axis_size("band")
    tile_count = lax.axis_size("tile")
    devices = band_count * tile_count
    blocks = weights.shape[0]
    day_count, members, _ = src_field.shape
    own_tiles = gamma_shape.shape[0] // 128
    capacity = max(2, 2 * blocks // devices)
    gathered = lax.all_gather(src_field, "tile", axis=2, tiled=True)
    gathered = gathered.reshape(day_count, members, -1, 128)
    chosen = jnp.take(gathered, block_slab, axis=2)
    pieces = jnp.einsum("dmbs,bst->bmt", chosen, weights, preferred_element_type=jnp.float32)
    owner_ids = block_dest[:, 0]
    slot_rank = rank_within(owner_ids, devices)
    position = owner_ids * capacity + slot_rank
    outgoing = jnp.zeros((devices * capacity, members, 128), jnp.float32).at[position].set(pieces)
    labels = (
        jnp.zeros((devices * capacity,), jnp.float32)
        .at[position]
        .set(block_tile.astype(jnp.float32))
    )
    packed = outgoing.reshape(band_count, tile_count * capacity, members, 128)
    tile_tags = labels.reshape(band_count, tile_count * capacity)
    arrived, arrived_tags = (
        lax.all_to_all(
            packed.astype(jnp.bfloat16), "band", split_axis=0, concat_axis=0, tiled=True
        ).astype(packed.dtype),
        lax.all_to_all(
            tile_tags.astype(jnp.bfloat16), "band", split_axis=0, concat_axis=0, tiled=True
        ).astype(tile_tags.dtype),
    )
    column = jnp.arange(tile_count * capacity, dtype=jnp.int32) // capacity
    target = column[None, :] * own_tiles + arrived_tags.astype(jnp.int32)
    band_partial = jax.ops.segment_sum(
        arrived.reshape(-1, members, 128), target.reshape(-1), num_segments=tile_count * own_tiles
    )
    summed = lax.psum_scatter(band_partial, "tile", scatter_dimension=0, tiled=True)
    remapped = jnp.transpose(summed, (1, 0, 2)).reshape(members, own_tiles * 128)
    season_total = prior_total + remapped
    shape_full = jnp.broadcast_to(gamma_shape[None, :], season_total.shape)
    probability = lower_gamma(shape_full, season_total / gamma_scale[None, :])
    probability = jnp.clip(probability, PROB_FLOOR, 1.0 - PROB_FLOOR)
    spi_index = normal_quantile(probability)
    return (season_total, spi_index)


def solution(mesh):
    placed = (
        P(None, None, ("band", "tile")),
        P(("band", "tile"), None, None),
        P(("band", "tile")),
        P(("band", "tile"), None),
        P(("band", "tile")),
        P(None, ("band", "tile")),
        P(("band", "tile")),
        P(("band", "tile")),
    )
    return jax.shard_map(
        shards,
        mesh=mesh,
        in_specs=placed,
        out_specs=(P(None, ("band", "tile")), P(None, ("band", "tile"))),
        check_vma=False,
    )
```

profile of v0, /device:TPU:1, one launch (start us, length us, event | category | flops | bytes accessed | tf_op | source)
XLA Modules:
  0.0 382.7 jit_solution(5081914653799887709)
XLA Ops:
  7.2 0.7 all-gather.2.cloned.1.call-update
  7.9 0.8 copy.17
  9.0 0.7 convert_element_type.80
  9.7 0.9 fusion.38
  10.6 0.7 compare_select_fusion
  11.3 1.4 scatter_custom_fusion
  12.7 0.7 convert_element_type.93
  13.4 13.1 %all-to-all-start = ((bf16[64,1,8]{2,1,0:T(2,128)(2,1)}), bf16[64,1,8]{2,1,0:T(2,128)(2,1)S(1)}, u32[]{:S(2)}, u32[]{:S(2)}) async-start(bf16[64,1,8]{2,1,0:T(2,128)(2,1)} %convert_element_type.93), calls=%async_computation | async-start | bytes 65536 | tf_op jit(solution)/shard_map/all_to_all | solution.py:118
  26.5 0.7 compare_select_fusion.1
  27.2 0.7 compare_and_fusion
  27.9 36.3 %all-gather.2.cloned.1.call-done = bf16[4,32,16384]{2,1,0:T(8,128)(2,1)} async-done(((bf16[4,32,4096]{2,1,0:T(8,128)(2,1)}), bf16[4,32,16384]{2,1,0:T(8,128)(2,1)}) %all-gather.2.cloned.1.call-update) | async-done | bytes 4194320 | tf_op jit(solution)/shard_map/all_gather | solution.py:99
  64.2 4.9 %copy_bitcast_fusion = bf16[4,32,128,128]{3,1,2,0:T(8,128)(2,1)} fusion(bf16[4,32,16384]{2,1,0:T(8,128)(2,1)} %all-gather.2.cloned.1.call-done), kind=kLoop, calls=%fused_computation.15 | loop fusion | bytes 8388608 | tf_op jit(solution)/shard_map/reshape | solution.py:100
  69.1 10.8 %gather_fusion = bf16[256,4,32,128]{3,2,1,0:T(8,128)(2,1)} fusion(bf16[4,32,128,128]{3,1,2,0:T(8,128)(2,1)} %copy_bitcast_fusion, s32[1024]{0:T(1024)S(1)} %pad_clamp_fusion), kind=kCustom, calls=%fused_computation | custom fusion | bytes 16778240 | tf_op jit(solution)/shard_map/jit(_take)/gather | solution.py:101
  79.9 5.2 %convert_reduce_fusion = bf16[256,32,128]{2,1,0:T(8,128)(2,1)S(1)} fusion(bf16[256,4,32,128]{3,2,1,0:T(8,128)(2,1)} %gather_fusion, pred[256]{0:T(512)(128)(4,1)S(1)} %compare_and_fusion), kind=kLoop, calls=%fused_computation.14 | loop fusion | flops 11534336 | bytes 10486016 | tf_op jit(solution)/shard_map/dmbs,bst->bmt/reduce_sum | solution.py:102
  85.1 7.7 %fusion.5 = f32[256,32,128]{2,1,0:T(8,128)} fusion(bf16[256,128,128]{2,1,0:T(8,128)(2,1)} %param.13, bf16[256,32,128]{2,1,0:T(8,128)(2,1)S(1)} %convert_reduce_fusion), kind=kOutput, calls=%fused_computation.17 | convolution fusion | flops 268435456 | bytes 14680064 | tf_op jit(solution)/shard_map/dmbs,bst->bmt/dot_general | solution.py:102
  92.8 4.3 %broadcast_in_dim.52 = f32[512,32,128]{2,1,0:T(8,128)} broadcast(f32[]{:T(128)} %constant.75.clone.1), dimensions={} | broadcast | bytes 8388612 | tf_op jit(solution)/shard_map/broadcast_in_dim | solution.py:106
  97.1 33.5 %scatter_fusion = f32[512,32,128]{2,1,0:T(8,128)} fusion(f32[512,32,128]{2,1,0:T(8,128)} %broadcast_in_dim.52, s32[256]{0:T(256)S(1)} %bitcast.46, f32[256,32,128]{2,1,0:T(8,128)} %fusion.5), kind=kCustom, calls=%fused_computation.2 | custom fusion | bytes 12583936 | tf_op jit(solution)/shard_map/scatter | solution.py:106
  130.6 6.4 %convert_element_type.87 = bf16[512,32,128]{2,1,0:T(8,128)(2,1)} convert(f32[512,32,128]{2,1,0:T(8,128)} %scatter_fusion) | non-fusion elementwise | flops 2097152 | bytes 12582912 | tf_op jit(solution)/shard_map/convert_element_type | solution.py:116
  137.0 11.2 %all-to-all-start.1 = ((bf16[64,8,32,128]{3,2,1,0:T(8,128)(2,1)}), bf16[64,8,32,128]{3,2,1,0:T(8,128)(2,1)}, u32[]{:S(2)}, u32[]{:S(2)}) async-start(bf16[64,8,32,128]{3,2,1,0:T(8,128)(2,1)} %bitcast.38), calls=%async_computation.1 | async-start | bytes 8388608 | tf_op jit(solution)/shard_map/all_to_all | solution.py:115
  148.5 94.3 %all-to-all-done.1 = bf16[64,8,32,128]{3,2,1,0:T(8,128)(2,1)} async-done(((bf16[64,8,32,128]{3,2,1,0:T(8,128)(2,1)}), bf16[64,8,32,128]{3,2,1,0:T(8,128)(2,1)}, u32[]{:S(2)}, u32[]{:S(2)}) %all-to-all-start.1) | async-done | bytes 4194336 | tf_op jit(solution)/shard_map/all_to_all | solution.py:115
  242.9 6.6 %bitcast_convert_fusion = f32[512,32,128]{2,1,0:T(8,128)} fusion(bf16[64,8,32,128]{3,2,1,0:T(8,128)(2,1)} %all-to-all-done.1), kind=kLoop, calls=%fused_computation.16 | loop fusion | flops 2097152 | bytes 12582912 | tf_op jit(solution)/shard_map/reshape | solution.py:125
  249.8 44.8 %scatter_fusion.1 = f32[128,32,128]{2,1,0:T(8,128)S(1)} fusion(f32[128,32,128]{2,1,0:T(8,128)S(1)} %broadcast_in_dim.50, s32[512]{0:T(512)S(1)} %bitcast.44, f32[512,32,128]{2,1,0:T(8,128)} %bitcast_convert_fusion), kind=kCustom, calls=%fused_computation.3 | custom fusion | flops 2097152 | bytes 25167872 | tf_op jit(solution)/shard_map/scatter-add | solution.py:124
  294.6 1.3 copy-done
  296.0 28.8 %reduce-scatter.2.cloned.1.call-done = f32[32,32,128]{2,1,0:T(8,128)} async-done(((f32[128,32,128]{2,1,0:T(8,128)}), f32[32,32,128]{2,1,0:T(8,128)}) %reduce-scatter.2.cloned.1.call-update) | async-done | bytes 524304 | tf_op jit(solution)/shard_map/reduce_scatter | solution.py:127
  324.8 1.3 broadcast_minimum_fusion
  326.3 32.6 %while.37 = (s32[]{:T(128)}, f32[32,4096]{1,0:T(8,128)S(1)}, f32[32,4096]{1,0:T(8,128)S(1)}, f32[32,4096]{1,0:T(8,128)S(1)}, f32[32,4096]{1,0:T(8,128)S(1)}, /*index=5*/f32[4096]{0:T(1024)S(1)}, s32[]{:T(128)}, s32[]{:T(128)}) while((s32[]{:T(128)}, f32[32,4096]{1,0:T(8,128)S(1)}, f32[32,4096]{1,0:T(8,128)S(1)}, ...), condition=%wide.region_11.12_spmd.clone, body=%wide.region_10.11_spmd.clone.sunk | while | flops 1187846 | bytes 4243591 | solution.py:78
  326.3 0.5 multiply_multiply_fusion.6
  326.9 0.5 multiply_multiply_fusion.6
  327.4 0.5 multiply_multiply_fusion.6
  327.9 0.5 multiply_multiply_fusion.6
  328.4 0.5 multiply_multiply_fusion.6
  328.9 0.5 multiply_multiply_fusion.6
  329.4 0.5 multiply_multiply_fusion.6
  329.9 0.5 multiply_multiply_fusion.6
  330.4 0.5 multiply_multiply_fusion.6
  330.9 0.5 multiply_multiply_fusion.6
  331.4 0.5 multiply_multiply_fusion.6
  331.9 0.5 multiply_multiply_fusion.6
  332.5 0.5 multiply_multiply_fusion.6
  333.0 0.5 multiply_multiply_fusion.6
  333.5 0.5 multiply_multiply_fusion.6
  334.5 0.5 multiply_multiply_fusion.6
  335.0 0.5 multiply_multiply_fusion.6
  336.0 0.5 multiply_multiply_fusion.6
  336.5 0.5 multiply_multiply_fusion.6
  338.1 0.5 multiply_multiply_fusion.6
  339.6 0.5 multiply_multiply_fusion.6
  341.1 0.5 multiply_multiply_fusion.6
  342.6 0.5 multiply_multiply_fusion.6
  344.2 0.5 multiply_multiply_fusion.6
  344.7 0.5 multiply_multiply_fusion.6
  345.7 0.5 multiply_multiply_fusion.6
  346.2 0.5 multiply_multiply_fusion.6
  347.7 0.5 multiply_multiply_fusion.6
  349.3 0.5 multiply_multiply_fusion.6
  350.8 0.5 multiply_multiply_fusion.6
  352.3 0.5 multiply_multiply_fusion.6
  353.9 0.5 multiply_multiply_fusion.6
  354.4 0.5 multiply_multiply_fusion.6
  355.4 0.5 multiply_multiply_fusion.6
  355.9 0.5 multiply_multiply_fusion.6
  357.4 0.5 multiply_multiply_fusion.6
  359.0 13.3 %while.36 = (s32[]{:T(128)}, f32[32,4096]{1,0:T(8,128)S(1)}, f32[32,4096]{1,0:T(8,128)S(1)}, f32[32,4096]{1,0:T(8,128)S(1)}, f32[4096]{0:T(1024)S(1)}, /*index=5*/s32[]{:T(128)}) while((s32[]{:T(128)}, f32[32,4096]{1,0:T(8,128)S(1)}, f32[32,4096]{1,0:T(8,128)S(1)}, f32[32,4096]{1,0:T(8,128)S(1)}, f32[4096]{0:T(1024)S(1)}, ...), condition=%wide.region_9.10_spmd.clone, body=%wide.region_8.9_spmd.clone.sunk | while | flops 397315 | bytes 2670673 | solution.py:64
  372.3 3.6 select_select_fusion
  (254 shorter events, 26.0 us)
Async XLA Ops:
  7.2 57.0 %all-gather.2.cloned.1.call-start = ((), (), s32[]{:S(2)}) async-start(), calls=%async_computation.3 | async-start | bytes 5242880 | tf_op jit(solution)/shard_map/all_gather | solution.py:99
  13.4 123.6 %all-to-all-start = ((bf16[64,1,8]{2,1,0:T(2,128)(2,1)}), bf16[64,1,8]{2,1,0:T(2,128)(2,1)S(1)}, u32[]{:S(2)}, u32[]{:S(2)}) async-start(bf16[64,1,8]{2,1,0:T(2,128)(2,1)} %convert_element_type.93), calls=%async_computation | async-start | bytes 65536 | tf_op jit(solution)/shard_map/all_to_all | solution.py:118
  137.0 105.9 %all-to-all-start.1 = ((bf16[64,8,32,128]{3,2,1,0:T(8,128)(2,1)}), bf16[64,8,32,128]{3,2,1,0:T(8,128)(2,1)}, u32[]{:S(2)}, u32[]{:S(2)}) async-start(bf16[64,8,32,128]{3,2,1,0:T(8,128)(2,1)} %bitcast.38), calls=%async_computation.1 | async-start | bytes 8388608 | tf_op jit(solution)/shard_map/all_to_all | solution.py:115
  148.1 176.7 %reduce-scatter.2.cloned.1.call-start = ((), (), s32[]{:S(2)}) async-start(), calls=%async_computation.4 | async-start | bytes 2621440 | tf_op jit(solution)/shard_map/reduce_scatter | solution.py:127
  249.7 46.3 %copy-start.1 = (f32[4096]{0:T(1024)S(1)}, f32[4096]{0:T(1024)}, u32[]{:S(2)}) copy-start(f32[4096]{0:T(1024)} %param.18) | copy-start | bytes 49156
  249.7 75.1 %copy-start.3 = (f32[4096]{0:T(1024)S(1)}, f32[4096]{0:T(1024)}, u32[]{:S(2)}) copy-start(f32[4096]{0:T(1024)} %param.19) | copy-start | bytes 49156
  294.6 1.4 copy-start
  326.1 46.2 %copy-start.2 = (f32[32,4096]{1,0:T(8,128)}, f32[32,4096]{1,0:T(8,128)S(1)}, u32[]{:S(2)}) copy-start(f32[32,4096]{1,0:T(8,128)S(1)} %get-tuple-element.273) | copy-start | bytes 1572868
Sparse Core Ops, SparseCore 0:
  9.8 54.3 all-gather.1
  296.1 28.6 reduce-scatter.1
where the time goes:
time: 385 us; the launch traced here: 383 us
  waiting for transfers between devices  160 us (42%)
  other arithmetic  114 us (30%)
  local copies, waits for them, and re-layouts  58.4 us (15%)
  starting transfers between devices  24.4 us (6%)
  between operations  14.3 us (4%)
  matrix products  7.66 us (2%)
  loops' own time  4.34 us (1%)
    all_to_all x1, waiting for transfers between devices, shards(): lax.all_to_all(packed.astype(jnp.bfloat16), 'band', split_axis=0, concat_...  94.3 us
    scatter-add x1, other arithmetic, shards(): jax.ops.segment_sum(arrived.reshape(-1, members, 128), target.reshape(-1)...  44.8 us
    all_gather x1, waiting for transfers between devices, shards(): gathered = lax.all_gather(src_field, 'tile', axis=2, tiled=True)  36.3 us
    scatter x1, local copies, waits for them, and re-layouts, shards(): jnp.zeros((devices * capacity, members, 128), jnp.float32).at[position]  33.5 us
    mul x64, other arithmetic, fraction_step(): return (denom_b, lentz_c, lentz_d, accum * lentz_d * lentz_c)  29.9 us
    reduce_scatter x1, waiting for transfers between devices, shards(): lax.psum_scatter(band_partial, 'tile', scatter_dimension=0, tiled=True)  28.8 us
    all_to_all x1, starting transfers between devices, shards(): lax.all_to_all(tile_tags.astype(jnp.bfloat16), 'band', split_axis=0, conc...  13.1 us
    all_to_all x1, starting transfers between devices, shards(): lax.all_to_all(packed.astype(jnp.bfloat16), 'band', split_axis=0, concat_...  11.2 us
  transfers between devices with their start and end apart: 4, of which 3 were waited for; matrix products, arithmetic and copies ran while one was open for 21% of the time, Pallas kernels for 0%

commit v1 on v0

--- a/solution.py
+++ b/solution.py
@@ -96,7 +96,9 @@
     day_count, members, _ = src_field.shape
     own_tiles = gamma_shape.shape[0] // 128
     capacity = max(2, 2 * blocks // devices)
-    gathered = lax.all_gather(src_field, "tile", axis=2, tiled=True)
+    gathered = jnp.concatenate(
+        lax.all_to_all(jnp.stack([src_field] * lax.axis_size("tile")), "tile", 0, 0), axis=2
+    )
     gathered = gathered.reshape(day_count, members, -1, 128)
     chosen = jnp.take(gathered, block_slab, axis=2)
     pieces = jnp.einsum("dmbs,bst->bmt", chosen, weights, preferred_element_type=jnp.float32)

time: 385 us -> 415 us (1.078)
  local copies, waits for them, and re-layouts: 58.4 us -> 79.3 us
  starting transfers between devices: 24.4 us -> 30.8 us
  waiting for transfers between devices: 160 us -> 166 us
    all_to_all x0 -> x1, waiting for transfers between devices: none -> 44.1 us  [shards(): lax.all_to_all(jnp.stack([src_field] * lax.axis_size('tile')), 'tile', 0, 0)]
    all_gather x1 -> x0, waiting for transfers between devices: 36.3 us -> none  [shards(): gathered = lax.all_gather(src_field, 'tile', axis=2, tiled=True)]
    another operation x3 -> x6, local copies, waits for them, and re-layouts: 0.03 us -> 19 us  [the longest x2 15.3 us: shards(): gathered = gathered.reshape(day_count, members, -1, 128)]
    all_to_all x0 -> x1, starting transfers between devices: none -> 4.99 us  [shards(): lax.all_to_all(jnp.stack([src_field] * lax.axis_size('tile')), 'tile', 0, 0)]
  transfers between devices with their start and end apart: 4 -> 4, of which waited for: 3 -> 3; matrix products, arithmetic and copies ran while one was open for 21% -> 23% of each run, Pallas kernels for 0% -> 0%
where the time goes in v1:
time: 415 us; the launch traced here: 413 us
  waiting for transfers between devices  166 us (40%)
  other arithmetic  110 us (27%)
  local copies, waits for them, and re-layouts  79.3 us (19%)
  starting transfers between devices  30.8 us (7%)
  between operations  14.3 us (3%)
  matrix products  7.66 us (2%)
  loops' own time  4.34 us (1%)
    all_to_all x1, waiting for transfers between devices, shards(): lax.all_to_all(packed.astype(jnp.bfloat16), 'band', split_axis=0, concat_...  94.3 us
    scatter-add x1, other arithmetic, shards(): jax.ops.segment_sum(arrived.reshape(-1, members, 128), target.reshape(-1)...  44.8 us
    all_to_all x1, waiting for transfers between devices, shards(): lax.all_to_all(jnp.stack([src_field] * lax.axis_size('tile')), 'tile', 0, 0)  44.1 us
    scatter x1, local copies, waits for them, and re-layouts, shards(): jnp.zeros((devices * capacity, members, 128), jnp.float32).at[position]  33.5 us
    mul x64, other arithmetic, fraction_step(): return (denom_b, lentz_c, lentz_d, accum * lentz_d * lentz_c)  29.9 us
    reduce_scatter x1, waiting for transfers between devices, shards(): lax.psum_scatter(band_partial, 'tile', scatter_dimension=0, tiled=True)  27.9 us
    all_to_all x1, starting transfers between devices, shards(): lax.all_to_all(tile_tags.astype(jnp.bfloat16), 'band', split_axis=0, conc...  15.4 us
    another operation x2, local copies, waits for them, and re-layouts, shards(): gathered = gathered.reshape(day_count, members, -1, 128)  15.3 us
  transfers between devices with their start and end apart: 4, of which 3 were waited for; matrix products, arithmetic and copies ran while one was open for 23% of the time, Pallas kernels for 0%

profile of v1, /device:TPU:1, one launch (start us, length us, event | category | flops | bytes accessed | tf_op | source)
XLA Modules:
  0.0 412.9 jit_solution(10610490001445541663)
XLA Ops:
  7.2 3.7 stack.2
  10.9 5.0 %all-to-all-start.1 = ((bf16[4,4,32,4096]{3,2,1,0:T(8,128)(2,1)}), bf16[4,4,32,4096]{3,2,1,0:T(8,128)(2,1)}, u32[]{:S(2)}, u32[]{:S(2)}) async-start(bf16[4,4,32,4096]{3,2,1,0:T(8,128)(2,1)} %stack.2), calls=%async_computation.1 | async-start | bytes 8388608 | tf_op jit(solution)/shard_map/all_to_all | solution.py:100
  16.5 1.4 scatter_custom_fusion
  18.0 0.7 convert_element_type.93
  18.7 44.1 %all-to-all-done.1 = bf16[4,4,32,4096]{3,2,1,0:T(8,128)(2,1)} async-done(((bf16[4,4,32,4096]{3,2,1,0:T(8,128)(2,1)}), bf16[4,4,32,4096]{3,2,1,0:T(8,128)(2,1)}, u32[]{:S(2)}, u32[]{:S(2)}) %all-to-all-start.1) | async-done | bytes 4194336 | tf_op jit(solution)/shard_map/all_to_all | solution.py:100
  62.8 15.4 %all-to-all-start = ((bf16[64,1,8]{2,1,0:T(2,128)(2,1)}), bf16[64,1,8]{2,1,0:T(2,128)(2,1)S(1)}, u32[]{:S(2)}, u32[]{:S(2)}) async-start(bf16[64,1,8]{2,1,0:T(2,128)(2,1)} %convert_element_type.93), calls=%async_computation | async-start | bytes 65536 | tf_op jit(solution)/shard_map/all_to_all | solution.py:120
  78.2 7.4 %copy.21 = bf16[4,32,4,4096]{3,2,1,0:T(4,128)(2,1)} copy(bf16[4,32,4,4096]{3,1,0,2:T(8,128)(2,1)} %bitcast.8) | data formatting | bytes 8388608 | tf_op jit(solution)/shard_map/reshape | solution.py:99
  85.6 8.4 %reshape_reshape.3 = bf16[4,32,128,128]{3,2,1,0:T(8,128)(2,1)} reshape(bf16[4,32,4,4096]{3,2,1,0:T(4,128)(2,1)} %copy.21) | data formatting | bytes 8388608 | tf_op jit(solution)/shard_map/reshape;reshape | solution.py:102
  94.0 6.9 %copy.22 = bf16[4,32,128,128]{3,1,2,0:T(8,128)(2,1)} copy(bf16[4,32,128,128]{3,2,1,0:T(8,128)(2,1)} %reshape_reshape.3) | data formatting | bytes 8388608 | tf_op jit(solution)/shard_map/reshape;reshape | solution.py:102
  100.9 10.8 %gather_fusion = bf16[256,4,32,128]{3,2,1,0:T(8,128)(2,1)} fusion(bf16[4,32,128,128]{3,1,2,0:T(8,128)(2,1)} %copy.22, s32[1024]{0:T(1024)S(1)} %pad_clamp_fusion), kind=kCustom, calls=%fused_computation | custom fusion | bytes 16778240 | tf_op jit(solution)/shard_map/jit(_take)/gather | solution.py:103
  111.7 5.2 %convert_reduce_fusion = bf16[256,32,128]{2,1,0:T(8,128)(2,1)S(1)} fusion(bf16[256,4,32,128]{3,2,1,0:T(8,128)(2,1)} %gather_fusion, pred[256]{0:T(512)(128)(4,1)S(1)} %compare_and_fusion), kind=kLoop, calls=%fused_computation.14 | loop fusion | flops 11534336 | bytes 10486016 | tf_op jit(solution)/shard_map/dmbs,bst->bmt/reduce_sum | solution.py:104
  116.9 7.7 %fusion.5 = f32[256,32,128]{2,1,0:T(8,128)} fusion(bf16[256,128,128]{2,1,0:T(8,128)(2,1)} %param.13, bf16[256,32,128]{2,1,0:T(8,128)(2,1)S(1)} %convert_reduce_fusion), kind=kOutput, calls=%fused_computation.16 | convolution fusion | flops 268435456 | bytes 14680064 | tf_op jit(solution)/shard_map/dmbs,bst->bmt/dot_general | solution.py:104
  124.6 4.3 %broadcast_in_dim.52 = f32[512,32,128]{2,1,0:T(8,128)} broadcast(f32[]{:T(128)} %constant.75.clone.1), dimensions={} | broadcast | bytes 8388612 | tf_op jit(solution)/shard_map/broadcast_in_dim | solution.py:108
  128.9 33.5 %scatter_fusion = f32[512,32,128]{2,1,0:T(8,128)} fusion(f32[512,32,128]{2,1,0:T(8,128)} %broadcast_in_dim.52, s32[256]{0:T(256)S(1)} %bitcast.42, f32[256,32,128]{2,1,0:T(8,128)} %fusion.5), kind=kCustom, calls=%fused_computation.2 | custom fusion | bytes 12583936 | tf_op jit(solution)/shard_map/scatter | solution.py:108
  162.4 6.4 %convert_element_type.87 = bf16[512,32,128]{2,1,0:T(8,128)(2,1)} convert(f32[512,32,128]{2,1,0:T(8,128)} %scatter_fusion) | non-fusion elementwise | flops 2097152 | bytes 12582912 | tf_op jit(solution)/shard_map/convert_element_type | solution.py:118
  168.8 10.4 %all-to-all-start.2 = ((bf16[64,8,32,128]{3,2,1,0:T(8,128)(2,1)}), bf16[64,8,32,128]{3,2,1,0:T(8,128)(2,1)}, u32[]{:S(2)}, u32[]{:S(2)}) async-start(bf16[64,8,32,128]{3,2,1,0:T(8,128)(2,1)} %bitcast.34), calls=%async_computation.2 | async-start | bytes 8388608 | tf_op jit(solution)/shard_map/all_to_all | solution.py:117
  179.6 94.3 %all-to-all-done.2 = bf16[64,8,32,128]{3,2,1,0:T(8,128)(2,1)} async-done(((bf16[64,8,32,128]{3,2,1,0:T(8,128)(2,1)}), bf16[64,8,32,128]{3,2,1,0:T(8,128)(2,1)}, u32[]{:S(2)}, u32[]{:S(2)}) %all-to-all-start.2) | async-done | bytes 4194336 | tf_op jit(solution)/shard_map/all_to_all | solution.py:117
  273.9 6.6 %bitcast_convert_fusion = f32[512,32,128]{2,1,0:T(8,128)} fusion(bf16[64,8,32,128]{3,2,1,0:T(8,128)(2,1)} %all-to-all-done.2), kind=kLoop, calls=%fused_computation.15 | loop fusion | flops 2097152 | bytes 12582912 | tf_op jit(solution)/shard_map/reshape | solution.py:127
  280.8 44.8 %scatter_fusion.1 = f32[128,32,128]{2,1,0:T(8,128)S(1)} fusion(f32[128,32,128]{2,1,0:T(8,128)S(1)} %broadcast_in_dim.50, s32[512]{0:T(512)S(1)} %bitcast.40, f32[512,32,128]{2,1,0:T(8,128)} %bitcast_convert_fusion), kind=kCustom, calls=%fused_computation.3 | custom fusion | flops 2097152 | bytes 25167872 | tf_op jit(solution)/shard_map/scatter-add | solution.py:126
  325.7 1.3 copy-done
  327.1 27.9 %reduce-scatter.2.cloned.1.call-done = f32[32,32,128]{2,1,0:T(8,128)} async-done(((f32[128,32,128]{2,1,0:T(8,128)}), f32[32,32,128]{2,1,0:T(8,128)}) %reduce-scatter.2.cloned.1.call-update) | async-done | bytes 524304 | tf_op jit(solution)/shard_map/reduce_scatter | solution.py:129
  355.0 1.3 broadcast_minimum_fusion
  356.5 32.6 %while.37 = (s32[]{:T(128)}, f32[32,4096]{1,0:T(8,128)S(1)}, f32[32,4096]{1,0:T(8,128)S(1)}, f32[32,4096]{1,0:T(8,128)S(1)}, f32[32,4096]{1,0:T(8,128)S(1)}, /*index=5*/f32[4096]{0:T(1024)S(1)}, s32[]{:T(128)}, s32[]{:T(128)}) while((s32[]{:T(128)}, f32[32,4096]{1,0:T(8,128)S(1)}, f32[32,4096]{1,0:T(8,128)S(1)}, ...), condition=%wide.region_11.12_spmd.clone, body=%wide.region_10.11_spmd.clone.sunk | while | flops 1187846 | bytes 4243591 | solution.py:78
  356.5 0.5 multiply_multiply_fusion.6
  357.1 0.5 multiply_multiply_fusion.6
  357.6 0.5 multiply_multiply_fusion.6
  358.1 0.5 multiply_multiply_fusion.6
  358.6 0.5 multiply_multiply_fusion.6
  359.1 0.5 multiply_multiply_fusion.6
  359.6 0.5 multiply_multiply_fusion.6
  360.1 0.5 multiply_multiply_fusion.6
  360.6 0.5 multiply_multiply_fusion.6
  361.1 0.5 multiply_multiply_fusion.6
  361.6 0.5 multiply_multiply_fusion.6
  362.1 0.5 multiply_multiply_fusion.6
  362.7 0.5 multiply_multiply_fusion.6
  363.2 0.5 multiply_multiply_fusion.6
  363.7 0.5 multiply_multiply_fusion.6
  364.2 0.5 multiply_multiply_fusion.6
  364.7 0.5 multiply_multiply_fusion.6
  365.2 0.5 multiply_multiply_fusion.6
  365.7 0.5 multiply_multiply_fusion.6
  366.2 0.5 multiply_multiply_fusion.6
  366.7 0.5 multiply_multiply_fusion.6
  367.8 0.5 multiply_multiply_fusion.6
  369.3 0.5 multiply_multiply_fusion.6
  370.8 0.5 multiply_multiply_fusion.6
  372.3 0.5 multiply_multiply_fusion.6
  373.9 0.5 multiply_multiply_fusion.6
  374.4 0.5 multiply_multiply_fusion.6
  375.4 0.5 multiply_multiply_fusion.6
  375.9 0.5 multiply_multiply_fusion.6
  377.4 0.5 multiply_multiply_fusion.6
  379.0 0.5 multiply_multiply_fusion.6
  380.5 0.5 multiply_multiply_fusion.6
  382.0 0.5 multiply_multiply_fusion.6
  383.5 0.5 multiply_multiply_fusion.6
  384.1 0.5 multiply_multiply_fusion.6
  385.1 0.5 multiply_multiply_fusion.6
  385.6 0.5 multiply_multiply_fusion.6
  387.1 0.5 multiply_multiply_fusion.6
  388.6 0.5 multiply_multiply_fusion.6
  389.2 13.3 %while.36 = (s32[]{:T(128)}, f32[32,4096]{1,0:T(8,128)S(1)}, f32[32,4096]{1,0:T(8,128)S(1)}, f32[32,4096]{1,0:T(8,128)S(1)}, f32[4096]{0:T(1024)S(1)}, /*index=5*/s32[]{:T(128)}) while((s32[]{:T(128)}, f32[32,4096]{1,0:T(8,128)S(1)}, f32[32,4096]{1,0:T(8,128)S(1)}, f32[32,4096]{1,0:T(8,128)S(1)}, f32[4096]{0:T(1024)S(1)}, ...), condition=%wide.region_9.10_spmd.clone, body=%wide.region_8.9_spmd.clone.sunk | while | flops 397315 | bytes 2670673 | solution.py:64
  402.5 3.6 select_select_fusion
  (262 shorter events, 24.9 us)
Async XLA Ops:
  10.9 5.0 %copy-start.4 = (s32[256,1]{0,1:T(1,128)S(1)}, s32[256,1]{0,1:T(1,128)}, u32[]{:S(2)}) copy-start(s32[256,1]{0,1:T(1,128)} %param.15) | copy-start | bytes 3076
  10.9 5.4 %copy-start.5 = (s32[256]{0:T(256)S(1)}, s32[256]{0:T(256)}, u32[]{:S(2)}) copy-start(s32[256]{0:T(256)} %param.16) | copy-start | bytes 3076
  10.9 7.8 %copy-start.6 = (s32[256]{0:T(256)S(1)}, s32[256]{0:T(256)}, u32[]{:S(2)}) copy-start(s32[256]{0:T(256)} %param.14) | copy-start | bytes 3076
  10.9 51.9 %all-to-all-start.1 = ((bf16[4,4,32,4096]{3,2,1,0:T(8,128)(2,1)}), bf16[4,4,32,4096]{3,2,1,0:T(8,128)(2,1)}, u32[]{:S(2)}, u32[]{:S(2)}) async-start(bf16[4,4,32,4096]{3,2,1,0:T(8,128)(2,1)} %stack.2), calls=%async_computation.1 | async-start | bytes 8388608 | tf_op jit(solution)/shard_map/all_to_all | solution.py:100
  62.8 106.0 %all-to-all-start = ((bf16[64,1,8]{2,1,0:T(2,128)(2,1)}), bf16[64,1,8]{2,1,0:T(2,128)(2,1)S(1)}, u32[]{:S(2)}, u32[]{:S(2)}) async-start(bf16[64,1,8]{2,1,0:T(2,128)(2,1)} %convert_element_type.93), calls=%async_computation | async-start | bytes 65536 | tf_op jit(solution)/shard_map/all_to_all | solution.py:120
  168.8 105.1 %all-to-all-start.2 = ((bf16[64,8,32,128]{3,2,1,0:T(8,128)(2,1)}), bf16[64,8,32,128]{3,2,1,0:T(8,128)(2,1)}, u32[]{:S(2)}, u32[]{:S(2)}) async-start(bf16[64,8,32,128]{3,2,1,0:T(8,128)(2,1)} %bitcast.34), calls=%async_computation.2 | async-start | bytes 8388608 | tf_op jit(solution)/shard_map/all_to_all | solution.py:117
  179.2 175.8 %reduce-scatter.2.cloned.1.call-start = ((), (), s32[]{:S(2)}) async-start(), calls=%async_computation.4 | async-start | bytes 2621440 | tf_op jit(solution)/shard_map/reduce_scatter | solution.py:129
  280.8 46.3 %copy-start.1 = (f32[4096]{0:T(1024)S(1)}, f32[4096]{0:T(1024)}, u32[]{:S(2)}) copy-start(f32[4096]{0:T(1024)} %param.18) | copy-start | bytes 49156
  280.8 74.2 %copy-start.3 = (f32[4096]{0:T(1024)S(1)}, f32[4096]{0:T(1024)}, u32[]{:S(2)}) copy-start(f32[4096]{0:T(1024)} %param.19) | copy-start | bytes 49156
  325.7 1.4 copy-start
  356.3 46.2 %copy-start.2 = (f32[32,4096]{1,0:T(8,128)}, f32[32,4096]{1,0:T(8,128)S(1)}, u32[]{:S(2)}) copy-start(f32[32,4096]{1,0:T(8,128)S(1)} %get-tuple-element.273) | copy-start | bytes 1572868
Sparse Core Ops, SparseCore 0:
  327.2 27.8 reduce-scatter.1
